TPU v7x, 32 devices: a whole 2x2x4 slice. The times are simulated.
32 devices in a mesh: cell: 8 (over y, x, core), narrow: 4 (over z).
Axes of the slice: x: 2, y: 2, z: 4, core: 2. Of those that a mesh axis runs over, the one named last changes fastest.
Arguments:
- snapshots: bfloat16 [4096, 4096], P('cell', 'narrow'), may hold values from -6 to 6
- cell_volume: float32 [4096], P('cell'), may hold values from 0.1 to 10
- mode_vectors: bfloat16 [4096, 512], P('narrow'), may hold values from -0.09375 to 0.09375
- mode_scale: float32 [512], replicated, may hold values from 0.25 to 4
- interp_weights: bfloat16 [4096, 4096], P('cell', 'narrow'), may hold values from -0.09375 to 0.09375
Outputs:
- gram_matrix: float32 [4096, 4096], P('cell', 'narrow')
- fields: bfloat16 [4096, 4096], P('cell', 'narrow')
All inputs are finite; a program needn't handle non-finite values.
Results may differ from a plain program's by a relative error of at most 0.0064.
Values may be sent and summed in bfloat16 or wider, within the bound.
A program may use at most 128 MiB of HBM per device.

v0:
```python
import jax
import jax.numpy as jnp
from jax import lax
from jax.sharding import PartitionSpec as P


def shards(snapshots, cell_volume, mode_vectors, mode_scale, interp_weights):
    f32, bf16 = (jnp.float32, jnp.bfloat16)
    n_cell, n_narrow = (lax.axis_size("cell"), lax.axis_size("narrow"))
    total_cells = snapshots.shape[0] * n_cell
    rows = interp_weights.shape[0]
    weighted = (snapshots.astype(f32) * cell_volume[:, None]).astype(bf16)
    partial_shapes = jnp.dot(snapshots, mode_vectors, preferred_element_type=f32)
    mode_shapes = lax.psum(partial_shapes, "narrow").astype(bf16)
    gathered = lax.all_gather(snapshots, "narrow", axis=1, tiled=True)
    scaled_shapes = (
        mode_shapes.astype(f32) * (cell_volume / total_cells)[:, None] * mode_scale[None, :]
    ).astype(bf16)
    partial_coeffs = lax.dot_general(
        gathered, scaled_shapes, (((0,), (0,)), ((), ())), preferred_element_type=f32
    ).astype(bf16)
    coeffs = lax.psum_scatter(partial_coeffs, "cell", scatter_dimension=0, tiled=True)
    partial_new = lax.dot_general(
        coeffs, interp_weights, (((0,), (0,)), ((), ())), preferred_element_type=f32
    )
    new_coeffs = lax.psum(partial_new, "cell").astype(bf16)
    fields = jnp.dot(mode_shapes, new_coeffs, preferred_element_type=f32).astype(bf16)
    partial_gram = (
        lax.dot_general(gathered, weighted, (((0,), (0,)), ((), ())), preferred_element_type=f32)
        / total_cells
    ).astype(bf16)
    gram = lax.psum_scatter(partial_gram, "cell", scatter_dimension=0, tiled=True)
    return (gram.astype(f32), fields)


def solution(mesh):
    return jax.shard_map(
        shards,
        mesh=mesh,
        in_specs=(P("cell", "narrow"), P("cell"), P("narrow", None), P(), P("cell", "narrow")),
        out_specs=(P("cell", "narrow"), P("cell", "narrow")),
        check_vma=False,
    )
```

profile of v0, /device:TPU:0, one launch (start us, length us, event | category | flops | bytes accessed | tf_op | source)
XLA Modules:
  0.0 281.6 jit_solution(1832069264775600661)
XLA Ops:
  7.2 0.0 copy-start
  7.2 0.0 copy-start.4
  7.2 0.0 copy-start.3
  7.2 0.0 all-gather.2.cloned.1.call-start
  7.2 0.7 all-gather.2.cloned.1.call-update
  7.9 0.0 reduce-scatter.5.cloned.1.call-start
  8.0 2.2 fusion.8
  10.2 0.0 copy-done.4
  10.3 74.8 %all-reduce.2 = bf16[512,512]{1,0:T(8,128)(2,1)S(1)} all-reduce(f32[512,512]{1,0:T(8,128)S(1)} %fusion.8), channel_id=1, replica_groups=mesh['cell'=8,'narrow'=4] {'narrow'}, use_global_device_ids=true, to_apply=%region_1.0 | all-reduce | flops 262144 | bytes 1572864 | tf_op jit(solution)/shard_map/psum | solution.py:14
  85.1 0.0 copy-start.1
  85.1 34.5 %all-gather.2.cloned.1.call-done = bf16[512,4096]{1,0:T(8,128)(2,1)} async-done(((bf16[512,1024]{1,0:T(8,128)(2,1)}), bf16[512,4096]{1,0:T(8,128)(2,1)}) %all-gather.2.cloned.1.call-update) | async-done | bytes 4194320 | tf_op jit(solution)/shard_map/all_gather | solution.py:15
  119.6 0.0 copy-done.3
  119.6 6.6 %fusion.1 = bf16[4096,512]{0,1:T(8,128)(2,1)} fusion(bf16[512,4096]{1,0:T(8,128)(2,1)} %all-gather.2.cloned.1.call-done, f32[512]{0:T(512)S(1)} %copy-done.3, f32[512]{0:T(512)S(1)} %broadcast_multiply_fusion, bf16[512,512]{1,0:T(8,128)(2,1)S(1)} %all-reduce.2), kind=kOutput, calls=%fused_computation.3 | convolution fusion | flops 2150629376 | bytes 8916992 | tf_op jit(solution)/shard_map/dot_general | solution.py:19
  126.2 0.0 copy-done.1
  126.2 0.0 copy-start.2
  126.2 0.0 reduce-scatter.5.cloned.1.call-update
  126.3 0.0 reduce-scatter.3.cloned.1.call-start
  126.3 1.1 copy-done.2
  127.5 9.1 %fusion = bf16[4096,1024]{0,1:T(8,128)(2,1)} fusion(bf16[512,4096]{1,0:T(8,128)(2,1)} %all-gather.2.cloned.1.call-done, bf16[512,1024]{1,0:T(8,128)(2,1)S(1)} %copy-done.2, f32[512]{0:T(512)S(1)} %copy-done.4), kind=kOutput, calls=%fused_computation.1 | convolution fusion | flops 4304928768 | bytes 13633536 | tf_op jit(solution)/shard_map/dot_general | solution.py:29
  136.6 0.0 reduce-scatter.3.cloned.1.call-update
  136.6 41.2 %reduce-scatter.5.cloned.1.call-done = bf16[512,512]{0,1:T(8,128)(2,1)} async-done(((bf16[4096,512]{0,1:T(8,128)(2,1)}), bf16[512,512]{0,1:T(8,128)(2,1)}) %reduce-scatter.5.cloned.1.call-update) | async-done | bytes 524304 | tf_op jit(solution)/shard_map/reduce_scatter | solution.py:22
  177.8 0.0 copy-done
  177.8 1.8 fusion.9
  179.5 72.9 %all-reduce.3 = bf16[512,1024]{1,0:T(8,128)(2,1)} all-reduce(f32[512,1024]{1,0:T(8,128)S(1)} %fusion.9), channel_id=1, replica_groups=mesh['cell'=8,'narrow'=4] {'cell'}, use_global_device_ids=true, to_apply=%region_3.0 | all-reduce | flops 524288 | bytes 3145728 | tf_op jit(solution)/shard_map/psum | solution.py:26
  252.5 3.1 %convolution_convert_fusion.1 = bf16[512,1024]{1,0:T(8,128)(2,1)} fusion(bf16[512,1024]{1,0:T(8,128)(2,1)} %all-reduce.3, bf16[512,512]{1,0:T(8,128)(2,1)} %copy-done.1), kind=kOutput, calls=%fused_computation.5 | convolution fusion | flops 537395200 | bytes 2621440 | tf_op jit(solution)/shard_map/dot_general | solution.py:27
  255.5 16.9 %reduce-scatter.3.cloned.1.call-done = bf16[512,1024]{0,1:T(8,128)(2,1)} async-done(((bf16[4096,1024]{0,1:T(8,128)(2,1)}), bf16[512,1024]{0,1:T(8,128)(2,1)}) %reduce-scatter.3.cloned.1.call-update) | async-done | bytes 1048592 | tf_op jit(solution)/shard_map/reduce_scatter | solution.py:32
  272.5 2.6 copy.7
  (1 shorter events, 0.0 us)
Async XLA Ops:
  7.2 170.6 %copy-start = (bf16[512,1024]{1,0:T(8,128)(2,1)S(1)}, bf16[512,1024]{1,0:T(8,128)(2,1)}, u32[]{:S(2)}) copy-start(bf16[512,1024]{1,0:T(8,128)(2,1)} %param.9) | copy-start | bytes 3145732
  7.2 3.1 %copy-start.4 = (f32[512]{0:T(512)S(1)}, f32[512]{0:T(512)}, u32[]{:S(2)}) copy-start(f32[512]{0:T(512)} %param.6) | copy-start | bytes 6148
  7.2 112.4 %copy-start.3 = (f32[512]{0:T(512)S(1)}, f32[512]{0:T(512)}, u32[]{:S(2)}) copy-start(f32[512]{0:T(512)} %param.8) | copy-start | bytes 6148
  7.2 112.4 %all-gather.2.cloned.1.call-start = ((), (), s32[]{:S(2)}) async-start(), calls=%async_computation.2 | async-start | bytes 5242880 | tf_op jit(solution)/shard_map/all_gather | solution.py:15
  7.9 169.9 %reduce-scatter.5.cloned.1.call-start = ((), (), s32[]{:S(2)}) async-start(), calls=%async_computation.4 | async-start | bytes 4718592 | tf_op jit(solution)/shard_map/reduce_scatter | solution.py:22
  85.1 41.2 %copy-start.1 = (bf16[512,512]{1,0:T(8,128)(2,1)}, bf16[512,512]{1,0:T(8,128)(2,1)S(1)}, u32[]{:S(2)}) copy-start(bf16[512,512]{1,0:T(8,128)(2,1)S(1)} %all-reduce.2) | copy-start | bytes 1572868
  126.2 1.2 copy-start.2
  126.3 146.2 %reduce-scatter.3.cloned.1.call-start = ((), (), s32[]{:S(2)}) async-start(), calls=%async_computation.3 | async-start | bytes 9437184 | tf_op jit(solution)/shard_map/reduce_scatter | solution.py:32
Sparse Core Ops, SparseCore 0:
  9.6 109.9 all-gather.1
  126.4 51.3 reduce-scatter.4
  181.3 91.1 reduce-scatter.2
where the time goes:
time: 282 us
  blocking collectives  148 us (52%)
  waiting for transfers between devices  93.3 us (33%)
  matrix products  22.8 us (8%)
  between operations  13.8 us (5%)
  local copies, waits for them, and re-layouts  3.74 us (1%)
    psum x1, blocking collectives, shards(): mode_shapes = lax.psum(partial_shapes, 'narrow').astype(bf16)  74.8 us
    psum x1, blocking collectives, shards(): new_coeffs = lax.psum(partial_new, 'cell').astype(bf16)  72.9 us
    reduce_scatter x1, waiting for transfers between devices, shards(): lax.psum_scatter(partial_coeffs, 'cell', scatter_dimension=0, tiled=True)  41.2 us
    all_gather x1, waiting for transfers between devices, shards(): gathered = lax.all_gather(snapshots, 'narrow', axis=1, tiled=True)  34.5 us
    reduce_scatter x1, waiting for transfers between devices, shards(): lax.psum_scatter(partial_gram, 'cell', scatter_dimension=0, tiled=True)  16.9 us
    dot_general x1, matrix products, shards(): lax.dot_general(gathered, weighted, (((0,), (0,)), ((), ())), preferred_e...  9.13 us
    dot_general x1, matrix products, shards(): lax.dot_general(gathered, scaled_shapes, (((0,), (0,)), ((), ())), prefer...  6.61 us
  transfers between devices with their start and end apart: 3, of which 3 were waited for; matrix products, arithmetic and copies ran while one was open for 6% of the time, Pallas kernels for 0%

commit v1 on v0

--- a/solution.py
+++ b/solution.py
@@ -23,7 +23,7 @@
     partial_new = lax.dot_general(
         coeffs, interp_weights, (((0,), (0,)), ((), ())), preferred_element_type=f32
     )
-    new_coeffs = lax.psum(partial_new, "cell").astype(bf16)
+    new_coeffs = jnp.sum(lax.all_gather(partial_new, "cell"), axis=0).astype(bf16)
     fields = jnp.dot(mode_shapes, new_coeffs, preferred_element_type=f32).astype(bf16)
     partial_gram = (
         lax.dot_general(gathered, weighted, (((0,), (0,)), ((), ())), preferred_element_type=f32)

time: 282 us -> 361 us (1.28)
  waiting for transfers between devices: 93.3 us -> 237 us
  blocking collectives: 148 us -> 74.8 us
  other arithmetic: 0.01 us -> 7.94 us
    all_gather x0 -> x1, waiting for transfers between devices: none -> 88.9 us  [shards(): lax.all_gather(partial_new, 'cell')]
    psum x1 -> x0, blocking collectives: 72.9 us -> none  [shards(): new_coeffs = lax.psum(partial_new, 'cell').astype(bf16)]
    reduce_scatter x1, waiting for transfers between devices: 16.9 us -> 71.6 us  [shards(): lax.psum_scatter(partial_gram, 'cell', scatter_dimension=0, tiled=True)]
    reduce_sum x0 -> x1, other arithmetic: none -> 7.94 us  [shards(): jnp.sum(lax.all_gather(partial_new, 'cell'), axis=0).astype(bf16)]
  transfers between devices with their start and end apart: 3 -> 4, of which waited for: 3 -> 4; matrix products, arithmetic and copies ran while one was open for 6% -> 5% of each run, Pallas kernels for 0% -> 0%
where the time goes in v1:
time: 361 us; the launch traced here: 360 us
  waiting for transfers between devices  237 us (66%)
  blocking collectives  74.8 us (21%)
  matrix products  22.8 us (6%)
  between operations  13.8 us (4%)
  other arithmetic  7.94 us (2%)
  local copies, waits for them, and re-layouts  3.73 us (1%)
    all_gather x1, waiting for transfers between devices, shards(): lax.all_gather(partial_new, 'cell')  88.9 us
    psum x1, blocking collectives, shards(): mode_shapes = lax.psum(partial_shapes, 'narrow').astype(bf16)  74.8 us
    reduce_scatter x1, waiting for transfers between devices, shards(): lax.psum_scatter(partial_gram, 'cell', scatter_dimension=0, tiled=True)  71.6 us
    reduce_scatter x1, waiting for transfers between devices, shards(): lax.psum_scatter(partial_coeffs, 'cell', scatter_dimension=0, tiled=True)  41.1 us
    all_gather x1, waiting for transfers between devices, shards(): gathered = lax.all_gather(snapshots, 'narrow', axis=1, tiled=True)  34.6 us
    dot_general x1, matrix products, shards(): lax.dot_general(gathered, weighted, (((0,), (0,)), ((), ())), preferred_e...  9.12 us
    reduce_sum x1, other arithmetic, shards(): jnp.sum(lax.all_gather(partial_new, 'cell'), axis=0).astype(bf16)  7.94 us
  transfers between devices with their start and end apart: 4, of which 4 were waited for; matrix products, arithmetic and copies ran while one was open for 5% of the time, Pallas kernels for 0%

profile of v1, /device:TPU:0, one launch (start us, length us, event | category | flops | bytes accessed | tf_op | source)
XLA Modules:
  0.0 360.2 jit_solution(1477269806382173936)
XLA Ops:
  7.2 0.0 copy-start
  7.2 0.0 copy-start.3
  7.2 0.0 copy-start.2
  7.2 0.0 all-gather.4.cloned.1.call-start
  7.2 0.7 all-gather.4.cloned.1.call-update
  7.9 0.0 reduce-scatter.5.cloned.1.call-start
  8.0 2.2 fusion.8
  10.2 0.0 copy-done.3
  10.3 74.8 %all-reduce.1 = bf16[512,512]{1,0:T(8,128)(2,1)S(1)} all-reduce(f32[512,512]{1,0:T(8,128)S(1)} %fusion.8), channel_id=1, replica_groups=mesh['cell'=8,'narrow'=4] {'narrow'}, use_global_device_ids=true, to_apply=%region_1.0 | all-reduce | flops 262144 | bytes 1572864 | tf_op jit(solution)/shard_map/psum | solution.py:14
  85.1 34.6 %all-gather.4.cloned.1.call-done = bf16[512,4096]{1,0:T(8,128)(2,1)} async-done(((bf16[512,1024]{1,0:T(8,128)(2,1)}), bf16[512,4096]{1,0:T(8,128)(2,1)}) %all-gather.4.cloned.1.call-update) | async-done | bytes 4194320 | tf_op jit(solution)/shard_map/all_gather | solution.py:15
  119.6 0.0 copy-done.2
  119.6 6.6 %fusion.1 = bf16[4096,512]{0,1:T(8,128)(2,1)} fusion(bf16[512,4096]{1,0:T(8,128)(2,1)} %all-gather.4.cloned.1.call-done, f32[512]{0:T(512)S(1)} %copy-done.2, f32[512]{0:T(512)S(1)} %broadcast_multiply_fusion, bf16[512,512]{1,0:T(8,128)(2,1)S(1)} %all-reduce.1), kind=kOutput, calls=%fused_computation.3 | convolution fusion | flops 2150629376 | bytes 8916992 | tf_op jit(solution)/shard_map/dot_general | solution.py:19
  126.2 0.0 copy-start.1
  126.2 0.0 reduce-scatter.5.cloned.1.call-update
  126.3 0.0 reduce-scatter.3.cloned.1.call-start
  126.3 1.1 copy-done.1
  127.5 9.1 %fusion = bf16[4096,1024]{0,1:T(8,128)(2,1)} fusion(bf16[512,4096]{1,0:T(8,128)(2,1)} %all-gather.4.cloned.1.call-done, bf16[512,1024]{1,0:T(8,128)(2,1)S(1)} %copy-done.1, f32[512]{0:T(512)S(1)} %copy-done.3), kind=kOutput, calls=%fused_computation.1 | convolution fusion | flops 4304928768 | bytes 13633536 | tf_op jit(solution)/shard_map/dot_general | solution.py:29
  136.6 0.0 reduce-scatter.3.cloned.1.call-update
  136.6 0.0 all-gather.6.cloned.1.call-start
  136.7 41.1 %reduce-scatter.5.cloned.1.call-done = bf16[512,512]{0,1:T(8,128)(2,1)} async-done(((bf16[4096,512]{0,1:T(8,128)(2,1)}), bf16[512,512]{0,1:T(8,128)(2,1)}) %reduce-scatter.5.cloned.1.call-update) | async-done | bytes 524304 | tf_op jit(solution)/shard_map/reduce_scatter | solution.py:22
  177.8 0.0 copy-done
  177.8 3.1 fusion.9
  180.9 0.0 all-gather.6.cloned.1.call-update
  180.9 71.6 %reduce-scatter.3.cloned.1.call-done = bf16[512,1024]{0,1:T(8,128)(2,1)} async-done(((bf16[4096,1024]{0,1:T(8,128)(2,1)}), bf16[512,1024]{0,1:T(8,128)(2,1)}) %reduce-scatter.3.cloned.1.call-update) | async-done | bytes 1048592 | tf_op jit(solution)/shard_map/reduce_scatter | solution.py:32
  252.5 2.6 copy.7
  255.1 88.9 %all-gather.6.cloned.1.call-done = f32[4096,1024]{1,0:T(8,128)} async-done(((f32[512,1024]{1,0:T(8,128)}), f32[4096,1024]{1,0:T(8,128)}) %all-gather.6.cloned.1.call-update) | async-done | bytes 16777232 | tf_op jit(solution)/shard_map/all_gather | solution.py:26
  344.0 7.9 %reduce_sum.9 = bf16[512,1024]{1,0:T(8,128)(2,1)S(1)} reduce(f32[8,512,1024]{2,1,0:T(8,128)} %bitcast.13, f32[]{:T(128)} %constant.6.clone.1), dimensions={0}, to_apply=%region_3.0 | reduce | flops 3670016 | bytes 17825796 | tf_op jit(solution)/shard_map/reduce_sum | solution.py:26
  352.0 1.7 convolution_convert_fusion.1
  (1 shorter events, 0.0 us)
Async XLA Ops:
  7.2 170.6 %copy-start = (bf16[512,1024]{1,0:T(8,128)(2,1)S(1)}, bf16[512,1024]{1,0:T(8,128)(2,1)}, u32[]{:S(2)}) copy-start(bf16[512,1024]{1,0:T(8,128)(2,1)} %param.9) | copy-start | bytes 3145732
  7.2 3.1 copy-start.3
  7.2 112.4 %copy-start.2 = (f32[512]{0:T(512)S(1)}, f32[512]{0:T(512)}, u32[]{:S(2)}) copy-start(f32[512]{0:T(512)} %param.8) | copy-start | bytes 6148
  7.2 112.4 %all-gather.4.cloned.1.call-start = ((), (), s32[]{:S(2)}) async-start(), calls=%async_computation.2 | async-start | bytes 5242880 | tf_op jit(solution)/shard_map/all_gather | solution.py:15
  7.9 169.8 %reduce-scatter.5.cloned.1.call-start = ((), (), s32[]{:S(2)}) async-start(), calls=%async_computation.4 | async-start | bytes 4718592 | tf_op jit(solution)/shard_map/reduce_scatter | solution.py:22
  126.2 1.2 copy-start.1
  126.3 126.3 %reduce-scatter.3.cloned.1.call-start = ((), (), s32[]{:S(2)}) async-start(), calls=%async_computation.3 | async-start | bytes 9437184 | tf_op jit(solution)/shard_map/reduce_scatter | solution.py:32
  136.6 207.4 %all-gather.6.cloned.1.call-start = ((), (), s32[]{:S(2)}) async-start(), calls=%async_computation.5 | async-start | bytes 18874368 | tf_op jit(solution)/shard_map/all_gather | solution.py:26
Sparse Core Ops, SparseCore 0:
  9.6 109.9 all-gather.3
  126.4 51.3 reduce-scatter.4
  181.2 71.2 reduce-scatter.2
  254.3 89.6 all-gather.5
